TPU v7x, 128 devices: a whole 4x4x4 slice. The times are simulated.
128 devices in a mesh: req: 16 (over z, y), mp: 8 (over x, core).
Axes of the slice: x: 4, y: 4, z: 4, core: 2. Of those that a mesh axis runs over, the one named last changes fastest.
Arguments:
- q_pre: bfloat16 [8192, 3072], P('req', 'mp'), may hold values from -64 to 64
- k_pre: bfloat16 [8192, 1024], P('req', 'mp'), may hold values from -64 to 64
- v_pre: bfloat16 [8192, 1024], P('req', 'mp'), may hold values from -12 to 12
- q_bias: float32 [3072], P('mp'), may hold values from -3 to 3
- k_bias: float32 [1024], P('mp'), may hold values from -3 to 3
- v_bias: float32 [1024], P('mp'), may hold values from -3 to 3
- segment_ids: int32 [8192], P('req'), may hold values from -1 to 63, as said below
- lengths: int32 [16, 4], replicated, may hold values from 64 to 128, as said below
- page_table: int32 [16, 4], replicated, may hold values from 0 to 63, as said below
- w_out: bfloat16 [3072, 5120], P('mp'), may hold values from -0.109375 to 0.109375
- residual: bfloat16 [8192, 5120], P('req'), may hold values from -4 to 4
- norm_gain: float32 [5120], replicated, may hold values from 0.1 to 1.9
- w_gate: bfloat16 [5120, 6912], P('req', 'mp'), may hold values from -0.078125 to 0.078125
- w_up: bfloat16 [5120, 6912], P('req', 'mp'), may hold values from -0.078125 to 0.078125
Outputs:
- hidden: bfloat16 [8192, 6912], P('req', 'mp')
- kv_cache: bfloat16 [64, 8, 128, 256], P('req', 'mp')
Inputs may be any that keep to these rules, and one draw needn't show every extreme that they name: Requests of block r lie in order from the block's first token, request j taking lengths[r, j] tokens; in every block one request has exactly 128 tokens. `segment_ids`: token t of block r carries r * 4 + j inside request j's run of tokens given by lengths, and -1 after the last request of its block. `page_table`: every page is named once; page p is held by req index p // 4; the requests of one block have pages held by different req indices.
All inputs are finite; a program needn't handle non-finite values.
Results may differ from a plain program's by a relative error of at most 0.019.
Values may be sent and summed in bfloat16 or wider, within the bound.
A program may use at most 128 MiB of HBM per device.

v0:
```python
import math
import jax
import jax.numpy as jnp
from jax import lax
from jax.sharding import PartitionSpec as P

HD = 128
PAGE = 128
REQS = 4
THETA = 1000000.0
EPS = 1e-06


def rotate(values, positions):
    half_dim = values.shape[-1] // 2
    frequencies = THETA ** (-jnp.arange(half_dim, dtype=jnp.float32) * (2.0 / values.shape[-1]))
    angles = positions[:, None] * frequencies[None, :]
    cosine = jnp.cos(angles)[:, None, :]
    sine_part = jnp.sin(angles)[:, None, :]
    first_half = values[..., :half_dim]
    second = values[..., half_dim:]
    return jnp.concatenate(
        [first_half * cosine - second * sine_part, second * cosine + first_half * sine_part],
        axis=-1,
    )


def normalize(resid_rows, summed, gain_row):
    state = resid_rows.astype(jnp.float32) + summed
    scale_row = lax.rsqrt(jnp.mean(state * state, axis=-1, keepdims=True) + EPS)
    return (state * scale_row * gain_row).astype(jnp.bfloat16)


def shards(
    q_pre,
    k_pre,
    v_pre,
    q_bias,
    k_bias,
    v_bias,
    segment_ids,
    lengths,
    page_table,
    w_out,
    residual,
    norm_gain,
    w_gate,
    w_up,
):
    me_req = lax.axis_index("req")
    groups_all = lax.axis_size("req")
    block_rows = q_pre.shape[0]
    kv_heads = k_pre.shape[1] // HD
    q_heads = q_pre.shape[1] // HD
    group_size = q_heads // kv_heads
    wg_full = lax.all_gather(w_gate, "req", axis=0, tiled=True)
    wu_full = lax.all_gather(w_up, "req", axis=0, tiled=True)
    own_lens = lax.dynamic_index_in_dim(lengths, me_req, 0, keepdims=False)
    own_pages = lax.dynamic_index_in_dim(page_table, me_req, 0, keepdims=False)
    own_owner = own_pages // REQS
    starts = jnp.cumsum(own_lens) - own_lens
    alive = segment_ids >= 0
    req_idx = jnp.clip(segment_ids - me_req * REQS, 0, REQS - 1)
    req_hit = req_idx[:, None] == jnp.arange(REQS)[None, :]
    row_start = jnp.sum(jnp.where(req_hit, starts[None, :], 0), axis=1)
    token = jnp.arange(block_rows, dtype=jnp.int32)
    positions = (token - row_start).astype(jnp.float32)
    keep = alive[:, None, None]
    queries = rotate(
        (q_pre.astype(jnp.float32) + q_bias).reshape(block_rows, q_heads, HD), positions
    )
    queries = jnp.where(keep, queries, 0.0).astype(jnp.bfloat16)
    keys = rotate((k_pre.astype(jnp.float32) + k_bias).reshape(block_rows, kv_heads, HD), positions)
    keys = jnp.where(keep, keys, 0.0).astype(jnp.bfloat16)
    values = (v_pre.astype(jnp.float32) + v_bias).reshape(block_rows, kv_heads, HD)
    values = jnp.where(keep, values, 0.0).astype(jnp.bfloat16)
    scale_factor = 1.0 / math.sqrt(HD)
    q_groups = queries.reshape(block_rows, kv_heads, group_size, HD)
    scores = (
        jnp.einsum("qhge,khe->hgqk", q_groups, keys, preferred_element_type=jnp.float32)
        * scale_factor
    )
    allowed = (
        (segment_ids[:, None] == segment_ids[None, :])
        & alive[None, :]
        & (token[None, :] <= token[:, None])
    )[None, None]
    row_max = jnp.max(jnp.where(allowed, scores, -1e30), axis=-1, keepdims=True)
    weights = jnp.where(allowed, jnp.exp(scores - row_max), 0.0)
    row_sum = jnp.sum(weights, axis=-1, keepdims=True)
    present = alive[None, None, :, None]
    probs = jnp.where(present, weights / jnp.where(present, row_sum, 1.0), 0.0).astype(jnp.bfloat16)
    attended = jnp.einsum("hgqk,khe->qhge", probs, values, preferred_element_type=jnp.float32)
    attended = attended.astype(jnp.bfloat16).reshape(block_rows, q_heads * HD)
    kv_rows = jnp.concatenate([keys, values], axis=-1)
    kv_rows = jnp.pad(kv_rows, ((0, PAGE), (0, 0), (0, 0)))
    slot = jnp.arange(PAGE, dtype=jnp.int32)
    pages = []
    for j in range(REQS):
        page = lax.dynamic_slice_in_dim(kv_rows, starts[j], PAGE, axis=0)
        page = jnp.where((slot < own_lens[j])[:, None, None], page, jnp.zeros((), jnp.bfloat16))
        pages.append(page)
    pages = jnp.stack(pages)
    to_owner = (own_owner[None, :] == jnp.arange(groups_all)[:, None]).astype(jnp.bfloat16)
    kv_send = jnp.einsum(
        "gj,jphc->gphc", to_owner, pages, preferred_element_type=jnp.float32
    ).astype(jnp.bfloat16)
    kv_in = lax.all_to_all(kv_send, "req", split_axis=0, concat_axis=0, tiled=True)
    hits = (
        page_table[None, :, :] == (me_req * REQS + jnp.arange(REQS, dtype=jnp.int32))[:, None, None]
    )
    page_select = jnp.sum(hits.astype(jnp.int32), axis=2).astype(jnp.bfloat16)
    cache_out = jnp.einsum(
        "ls,sphc->lhpc", page_select, kv_in, preferred_element_type=jnp.float32
    ).astype(jnp.bfloat16)
    summed = lax.psum(
        jnp.dot(attended, w_out, preferred_element_type=jnp.float32).astype(jnp.bfloat16), "mp"
    ).astype(jnp.float32)
    normed = normalize(residual, summed, norm_gain)
    gate_acc = jnp.dot(normed, wg_full, preferred_element_type=jnp.float32)
    up_acc = jnp.dot(normed, wu_full, preferred_element_type=jnp.float32)
    hidden = (jax.nn.silu(gate_acc) * up_acc).astype(jnp.bfloat16)
    return (hidden, cache_out)


def solution(mesh):
    in_specs = (
        P("req", "mp"),
        P("req", "mp"),
        P("req", "mp"),
        P("mp"),
        P("mp"),
        P("mp"),
        P("req"),
        P(),
        P(),
        P("mp", None),
        P("req", None),
        P(),
        P("req", "mp"),
        P("req", "mp"),
    )
    out_specs = (P("req", "mp"), P("req", "mp", None, None))
    return jax.shard_map(shards, mesh=mesh, in_specs=in_specs, out_specs=out_specs, check_vma=False)
```

profile of v0, /device:TPU:1, one launch (start us, length us, event | category | flops | bytes accessed | tf_op | source)
XLA Modules:
  0.0 211.2 jit_solution(10629385373972112505)
XLA Ops:
  8.0 0.0 all-reduce.3.cloned.1.call-start
  8.1 0.9 fusion.45
  9.0 0.1 copy.96
  9.0 0.2 reduce-window.4
  9.2 0.7 broadcast_compare_fusion
  9.9 0.7 subtract_clamp_fusion
  10.6 0.1 select_reduce_fusion
  10.7 1.2 copy.81
  11.9 0.5 multiply_cosine_fusion.1
  12.4 0.9 add_bitcast_fusion
  13.3 1.2 fusion.28
  14.6 1.0 fusion.15
  15.6 0.0 copy-start.1
  15.6 0.0 copy-start.3
  15.6 0.8 convert_add_fusion.1
  16.4 0.1 multiply_subtract_fusion
  16.6 0.8 fusion
  17.4 0.7 fusion.3
  18.1 0.0 copy-done.1
  18.1 0.0 copy-done.3
  18.1 0.0 copy-start
  18.1 1.2 fusion.9
  19.3 0.9 copy-done
  20.2 4.7 %convolution_convert_fusion = bf16[512,5120]{1,0:T(8,128)(2,1)} fusion(bf16[512,384]{0,1:T(8,128)(2,1)S(1)} %bitcast.97, bf16[384,5120]{1,0:T(8,128)(2,1)S(1)} %copy-done), kind=kOutput, calls=%fused_computation.3 | convolution fusion | flops 2015887360 | bytes 9568256 | tf_op jit(solution)/shard_map/dot_general | solution.py:117
  24.9 0.0 all-reduce.3.cloned.1.call-update
  25.0 0.0 copy-start.2
  25.0 0.0 all-gather.3.cloned.1.call-start
  25.0 0.5 all-gather.3.cloned.1.call-update
  25.6 0.0 all-gather.5.cloned.1.call-start
  25.6 0.5 all-gather.5.cloned.1.call-update
  26.2 0.7 fusion.60
  34.6 0.7 fusion.59
  35.3 0.6 iota_compare_fusion.4
  35.9 0.7 iota_compare_fusion.5
  36.6 0.6 iota_compare_fusion.6
  37.3 0.7 iota_compare_fusion.7
  37.9 0.2 fusion.31
  38.1 0.1 fusion.43
  38.3 0.1 select_bitcast_fusion.3
  38.4 0.1 copy.85
  38.5 0.1 copy.86
  38.6 0.1 copy.87
  38.8 0.1 copy.88
  38.9 0.9 fusion.8
  39.8 1.4 copy.89
  41.2 8.6 %all-to-all-start = ((bf16[16,128,1,256]{3,1,2,0:T(8,128)(2,1)}), bf16[16,128,1,256]{3,1,2,0:T(8,128)(2,1)S(1)}, u32[]{:S(2)}, u32[]{:S(2)}) async-start(bf16[16,128,1,256]{3,1,2,0:T(8,128)(2,1)} %copy.89), calls=%async_computation | async-start | bytes 2097152 | tf_op jit(solution)/shard_map/all_to_all | solution.py:108
  49.8 0.0 copy-done.2
  49.8 0.1 convert_reduce_fusion
  49.9 18.8 %all-to-all-done = bf16[16,128,1,256]{3,1,2,0:T(8,128)(2,1)S(1)} async-done(((bf16[16,128,1,256]{3,1,2,0:T(8,128)(2,1)}), bf16[16,128,1,256]{3,1,2,0:T(8,128)(2,1)S(1)}, u32[]{:S(2)}, u32[]{:S(2)}) %all-to-all-start) | async-done | bytes 1048608 | tf_op jit(solution)/shard_map/all_to_all | solution.py:108
  68.7 0.7 fusion.12
  69.4 0.7 copy.91
  70.1 0.0 copy-start.4
  70.1 35.0 %all-reduce.3.cloned.1.call-done = bf16[512,5120]{1,0:T(8,128)(2,1)} async-done(((bf16[512,5120]{1,0:T(8,128)(2,1)}), bf16[512,5120]{1,0:T(8,128)(2,1)}) %all-reduce.3.cloned.1.call-update) | async-done | bytes 5242896 | tf_op jit(solution)/shard_map/psum | solution.py:116
  105.2 5.8 %multiply_reduce_fusion = f32[512]{0:T(512)S(1)} fusion(bf16[512,5120]{1,0:T(8,128)(2,1)} %all-reduce.3.cloned.1.call-done, bf16[512,5120]{1,0:T(8,128)(2,1)} %param.24), kind=kLoop, calls=%fused_computation.1 | loop fusion | flops 13106688 | bytes 10487808 | tf_op jit(solution)/shard_map/reduce_sum | solution.py:30
  111.0 3.9 %all-gather.3.cloned.1.call-done = bf16[5120,864]{1,0:T(8,128)(2,1)} async-done(((bf16[320,864]{1,0:T(8,128)(2,1)}), bf16[5120,864]{1,0:T(8,128)(2,1)}) %all-gather.3.cloned.1.call-update) | async-done | bytes 8847376 | tf_op jit(solution)/shard_map/all_gather | solution.py:56
  114.9 0.0 copy-done.4
  114.9 12.1 %fusion.58 = f32[512,864]{0,1:T(8,128)S(1)} fusion(bf16[5120,864]{1,0:T(8,128)(2,1)} %all-gather.3.cloned.1.call-done, bf16[512,5120]{1,0:T(8,128)(2,1)} %all-reduce.3.cloned.1.call-done, bf16[512,5120]{1,0:T(8,128)(2,1)} %param.24, f32[5120]{0:T(1024)S(1)} %copy-done.4, f32[512]{0:T(512)S(1)} %add_rsqrt_fusion), kind=kOutput, calls=%fused_computation.105 | convolution fusion | flops 4545576960 | bytes 21125120 | tf_op jit(solution)/shard_map/dot_general | solution.py:120
  127.0 64.0 %all-gather.5.cloned.1.call-done = bf16[5120,864]{1,0:T(8,128)(2,1)} async-done(((bf16[320,864]{1,0:T(8,128)(2,1)}), bf16[5120,864]{1,0:T(8,128)(2,1)}) %all-gather.5.cloned.1.call-update) | async-done | bytes 8847376 | tf_op jit(solution)/shard_map/all_gather | solution.py:57
  191.0 12.7 %multiply_convert_fusion.1 = bf16[512,864]{0,1:T(8,128)(2,1)} fusion(f32[512,864]{0,1:T(8,128)S(1)} %fusion.58, bf16[5120,864]{1,0:T(8,128)(2,1)} %all-gather.5.cloned.1.call-done, bf16[512,5120]{1,0:T(8,128)(2,1)} %all-reduce.3.cloned.1.call-done, bf16[512,5120]{1,0:T(8,128)(2,1)} %param.24, f32[5120]{0:T(1024)S(1)} %copy-done.4, f32[512]{0:T(512)S(1)} %add_rsqrt_fusion), kind=kOutput, calls=%fused_computation.11 | convolution fusion | flops 4548231168 | bytes 22009856 | tf_op jit(solution)/shard_map/dot_general | solution.py:121
  (8 shorter events, 0.1 us)
Async XLA Ops:
  8.0 97.2 %all-reduce.3.cloned.1.call-start = ((), (), s32[]{:S(2)}) async-start(), calls=%async_computation.1 | async-start | bytes 10485760 | tf_op jit(solution)/shard_map/psum | solution.py:116
  15.6 2.5 %copy-start.1 = (bf16[512,128]{1,0:T(8,128)(2,1)S(1)}, bf16[512,128]{1,0:T(8,128)(2,1)}, u32[]{:S(2)}) copy-start(bf16[512,128]{1,0:T(8,128)(2,1)} %param.16) | copy-start | bytes 393220
  15.6 2.5 %copy-start.3 = (f32[128]{0:T(128)S(1)}, f32[128]{0:T(128)}, u32[]{:S(2)}) copy-start(f32[128]{0:T(128)} %param.19) | copy-start | bytes 1540
  18.1 2.1 %copy-start = (bf16[384,5120]{1,0:T(8,128)(2,1)S(1)}, bf16[384,5120]{1,0:T(8,128)(2,1)}, u32[]{:S(2)}) copy-start(bf16[384,5120]{1,0:T(8,128)(2,1)} %param.23) | copy-start | bytes 11796484
  25.0 24.8 %copy-start.2 = (s32[16,4]{0,1:T(4,128)S(1)}, s32[16,4]{0,1:T(4,128)}, u32[]{:S(2)}) copy-start(s32[16,4]{0,1:T(4,128)} %param.22) | copy-start | bytes 772
  25.0 89.9 %all-gather.3.cloned.1.call-start = ((), (), s32[]{:S(2)}) async-start(), calls=%async_computation.2 | async-start | bytes 9748480 | tf_op jit(solution)/shard_map/all_gather | solution.py:56
  25.6 165.4 %all-gather.5.cloned.1.call-start = ((), (), s32[]{:S(2)}) async-start(), calls=%async_computation.3 | async-start | bytes 9748480 | tf_op jit(solution)/shard_map/all_gather | solution.py:57
  41.2 27.5 %all-to-all-start = ((bf16[16,128,1,256]{3,1,2,0:T(8,128)(2,1)}), bf16[16,128,1,256]{3,1,2,0:T(8,128)(2,1)S(1)}, u32[]{:S(2)}, u32[]{:S(2)}) async-start(bf16[16,128,1,256]{3,1,2,0:T(8,128)(2,1)} %copy.89), calls=%async_computation | async-start | bytes 2097152 | tf_op jit(solution)/shard_map/all_to_all | solution.py:108
  70.1 44.8 %copy-start.4 = (f32[5120]{0:T(1024)S(1)}, f32[5120]{0:T(1024)}, u32[]{:S(2)}) copy-start(f32[5120]{0:T(1024)} %param.25) | copy-start | bytes 61444
Sparse Core Ops, SparseCore 0:
  25.1 80.0 all-reduce.2
Sparse Core Ops, SparseCore 1:
  27.6 87.3 all-gather.2
  116.9 74.0 all-gather.4
where the time goes:
time: 212 us; the launch traced here: 211 us
  waiting for transfers between devices  123 us (58%)
  matrix products  33.1 us (16%)
  between operations  23.5 us (11%)
  other arithmetic  16.9 us (8%)
  starting transfers between devices  8.73 us (4%)
  local copies, waits for them, and re-layouts  6.03 us (3%)
    all_gather x1, waiting for transfers between devices, shards(): wu_full = lax.all_gather(w_up, 'req', axis=0, tiled=True)  64 us
    psum x1, waiting for transfers between devices, shards(): lax.psum(jnp.dot(attended, w_out, preferred_element_type=jnp.float32).ast...  35 us
    all_to_all x1, waiting for transfers between devices, shards(): lax.all_to_all(kv_send, 'req', split_axis=0, concat_axis=0, tiled=True)  18.8 us
    dot_general x1, matrix products, shards(): up_acc = jnp.dot(normed, wu_full, preferred_element_type=jnp.float32)  12.7 us
    dot_general x1, matrix products, shards(): gate_acc = jnp.dot(normed, wg_full, preferred_element_type=jnp.float32)  12.1 us
    all_to_all x1, starting transfers between devices, shards(): lax.all_to_all(kv_send, 'req', split_axis=0, concat_axis=0, tiled=True)  8.61 us
    reduce_sum x1, other arithmetic, normalize(): scale_row = lax.rsqrt(jnp.mean(state * state, axis=-1, keepdims=True) + EPS)  5.83 us
    dot_general x1, matrix products, shards(): jnp.dot(attended, w_out, preferred_element_type=jnp.float32)  4.72 us
  transfers between devices with their start and end apart: 4, of which 4 were waited for; matrix products, arithmetic and copies ran while one was open for 13% of the time, Pallas kernels for 0%

commit v1 on v0

--- a/solution.py
+++ b/solution.py
@@ -47,6 +47,22 @@
     w_gate,
     w_up,
 ):
+
+    def group_the_forms(vals, across="req"):
+        shares = jax.lax.axis_size(across)
+        runs = list(map(lambda dev_j: (dev_j, (dev_j + 1) % shares), range(shares)))
+        all_rows = list(map(lambda dev_j: (dev_j, (dev_j - 1) % shares), range(shares)))
+        right_arr, back = ([vals], [vals])
+        for _ in range(shares // 2):
+            right_arr.append(jax.lax.ppermute(right_arr[-1], axis_name=across, perm=runs))
+        for _ in range((shares - 1) // 2):
+            back.append(jax.lax.ppermute(back[-1], perm=all_rows, axis_name=across))
+        return jnp.roll(
+            jnp.concatenate([*right_arr[::-1], *back[1:]], 0),
+            (jax.lax.axis_index(across) - shares // 2) * vals.shape[0],
+            axis=0,
+        )
+
     me_req = lax.axis_index("req")
     groups_all = lax.axis_size("req")
     block_rows = q_pre.shape[0]
@@ -54,7 +70,7 @@
     q_heads = q_pre.shape[1] // HD
     group_size = q_heads // kv_heads
     wg_full = lax.all_gather(w_gate, "req", axis=0, tiled=True)
-    wu_full = lax.all_gather(w_up, "req", axis=0, tiled=True)
+    wu_full = group_the_forms(w_up)
     own_lens = lax.dynamic_index_in_dim(lengths, me_req, 0, keepdims=False)
     own_pages = lax.dynamic_index_in_dim(page_table, me_req, 0, keepdims=False)
     own_owner = own_pages // REQS

time: 212 us -> 285 us (1.34); the launches traced: 211 us -> 281 us
  local copies, waits for them, and re-layouts: 6.03 us -> 53.1 us
  starting transfers between devices: 8.73 us -> 45.4 us
  waiting for transfers between devices: 123 us -> 107 us
    ppermute x0 -> x15, waiting for transfers between devices: none -> 107 us  [the longest x7 58.6 us: group_the_forms(): back.append(jax.lax.ppermute(back[-1], perm=all_rows, axis_name=across))]
    all_gather x1 -> x0, waiting for transfers between devices: 64 us -> none  [shards(): wu_full = lax.all_gather(w_up, 'req', axis=0, tiled=True)]
    unnamed x13 -> x50, local copies, waits for them, and re-layouts: 2.92 us -> 49.1 us
    ppermute x0 -> x15, starting transfers between devices: none -> 39.2 us  [the longest x7 37 us: group_the_forms(): back.append(jax.lax.ppermute(back[-1], perm=all_rows, axis_name=across))]
    psum x1, waiting for transfers between devices: 35 us -> 0.01 us  [shards(): lax.psum(jnp.dot(attended, w_out, preferred_element_type=jnp.float32).ast...]
    all_to_all x1, waiting for transfers between devices: 18.8 us -> 0.01 us  [shards(): lax.all_to_all(kv_send, 'req', split_axis=0, concat_axis=0, tiled=True)]
    all_gather x1, waiting for transfers between devices: 3.88 us -> 0.01 us  [shards(): wg_full = lax.all_gather(w_gate, 'req', axis=0, tiled=True)]
  transfers between devices with their start and end apart: 4 -> 18, of which waited for: 4 -> 11; matrix products, arithmetic and copies ran while one was open for 13% -> 22% of each run, Pallas kernels for 0% -> 0%
where the time goes in v1:
time: 285 us; the launch traced here: 281 us
  waiting for transfers between devices  107 us (38%)
  local copies, waits for them, and re-layouts  53.1 us (19%)
  starting transfers between devices  45.4 us (16%)
  matrix products  34.7 us (12%)
  between operations  23.4 us (8%)
  other arithmetic  17.1 us (6%)
    ppermute x7, waiting for transfers between devices, group_the_forms(): back.append(jax.lax.ppermute(back[-1], perm=all_rows, axis_name=across))  58.6 us
    unnamed x50, local copies, waits for them, and re-layouts  49.1 us
    ppermute x8, waiting for transfers between devices, group_the_forms(): jax.lax.ppermute(right_arr[-1], axis_name=across, perm=runs)  48.1 us
    ppermute x7, starting transfers between devices, group_the_forms(): back.append(jax.lax.ppermute(back[-1], perm=all_rows, axis_name=across))  37 us
    dot_general x1, matrix products, shards(): up_acc = jnp.dot(normed, wu_full, preferred_element_type=jnp.float32)  13.4 us
    dot_general x1, matrix products, shards(): gate_acc = jnp.dot(normed, wg_full, preferred_element_type=jnp.float32)  12.1 us
    all_to_all x1, starting transfers between devices, shards(): lax.all_to_all(kv_send, 'req', split_axis=0, concat_axis=0, tiled=True)  6.16 us
    reduce_sum x1, other arithmetic, normalize(): scale_row = lax.rsqrt(jnp.mean(state * state, axis=-1, keepdims=True) + EPS)  5.83 us
  transfers between devices with their start and end apart: 18, of which 11 were waited for; matrix products, arithmetic and copies ran while one was open for 22% of the time, Pallas kernels for 0%

profile of v1, /device:TPU:1, one launch (start us, length us, event | category | flops | bytes accessed | tf_op | source)
XLA Modules:
  0.0 280.9 jit_solution(3184619685019200088)
XLA Ops:
  8.1 0.9 fusion.49
  10.7 1.2 copy.81
  12.4 1.2 add_bitcast_fusion
  13.6 1.2 fusion.32
  14.9 1.0 fusion.19
  18.4 2.1 fusion.13
  20.5 4.7 %convolution_convert_fusion = bf16[512,5120]{1,0:T(8,128)(2,1)} fusion(bf16[512,384]{0,1:T(8,128)(2,1)S(1)} %bitcast.96, bf16[384,5120]{1,0:T(8,128)(2,1)S(1)} %copy-done), kind=kOutput, calls=%fused_computation.5 | convolution fusion | flops 2015887360 | bytes 9568256 | tf_op jit(solution)/shard_map/dot_general | solution.py:133
  25.8 2.2 collective-permute-start
  28.0 17.6 %collective-permute-done = bf16[320,864]{1,0:T(8,128)(2,1)S(1)} collective-permute-done((bf16[320,864]{1,0:T(8,128)(2,1)S(1)}, bf16[320,864]{1,0:T(8,128)(2,1)S(1)}, u32[]{:S(2)}, u32[]{:S(2)}) %collective-permute-start) | collective-permute-done | bytes 552992 | tf_op jit(solution)/shard_map/ppermute | solution.py:57
  45.6 4.8 %collective-permute-start.8 = (bf16[320,864]{1,0:T(8,128)(2,1)S(1)}, bf16[320,864]{1,0:T(8,128)(2,1)S(1)}, u32[]{:S(2)}, u32[]{:S(2)}) collective-permute-start(bf16[320,864]{1,0:T(8,128)(2,1)S(1)} %copy-done.1), channel_id=1, source_target_pairs={{0,120},{8,0},{16,8},{24,16},{32,24},{40,32},{48,40},{56,48},{64,5... | collective-permute-start | bytes 1658888 | tf_op jit(solution)/shard_map/ppermute | solution.py:59
  50.4 18.1 %collective-permute-done.1 = bf16[320,864]{1,0:T(8,128)(2,1)S(1)} collective-permute-done((bf16[320,864]{1,0:T(8,128)(2,1)S(1)}, bf16[320,864]{1,0:T(8,128)(2,1)S(1)}, u32[]{:S(2)}, u32[]{:S(2)}) %collective-permute-start.1) | collective-permute-done | bytes 552992 | tf_op jit(solution)/shard_map/ppermute | solution.py:57
  79.3 4.9 %collective-permute-start.9 = (bf16[320,864]{1,0:T(8,128)(2,1)S(1)}, bf16[320,864]{1,0:T(8,128)(2,1)}, u32[]{:S(2)}, u32[]{:S(2)}) collective-permute-start(bf16[320,864]{1,0:T(8,128)(2,1)S(1)} %collective-permute-done.8), channel_id=1, source_target_pairs={{0,120},{8,0},{16,8},{24,16},{32,24},{40,32},{48,40},{56,48},{64,5... | collective-permute-start | bytes 1658888 | tf_op jit(solution)/shard_map/ppermute | solution.py:59
  84.1 4.0 %collective-permute-done.2 = bf16[320,864]{1,0:T(8,128)(2,1)S(1)} collective-permute-done((bf16[320,864]{1,0:T(8,128)(2,1)S(1)}, bf16[320,864]{1,0:T(8,128)(2,1)S(1)}, u32[]{:S(2)}, u32[]{:S(2)}) %collective-permute-start.2) | collective-permute-done | bytes 552992 | tf_op jit(solution)/shard_map/ppermute | solution.py:57
  89.2 19.4 %collective-permute-done.9 = bf16[320,864]{1,0:T(8,128)(2,1)} collective-permute-done((bf16[320,864]{1,0:T(8,128)(2,1)S(1)}, bf16[320,864]{1,0:T(8,128)(2,1)}, u32[]{:S(2)}, u32[]{:S(2)}) %collective-permute-start.9) | collective-permute-done | bytes 552992 | tf_op jit(solution)/shard_map/ppermute | solution.py:59
  108.6 5.6 %collective-permute-start.10 = (bf16[320,864]{1,0:T(8,128)(2,1)}, bf16[320,864]{1,0:T(8,128)(2,1)}, u32[]{:S(2)}, u32[]{:S(2)}) collective-permute-start(bf16[320,864]{1,0:T(8,128)(2,1)} %collective-permute-done.9), channel_id=1, source_target_pairs={{0,120},{8,0},{16,8},{24,16},{32,24},{40,32},{48,40},{56,48},{64,5... | collective-permute-start | bytes 1658888 | tf_op jit(solution)/shard_map/ppermute | solution.py:59
  114.2 2.7 collective-permute-done.3
  117.5 0.9 fusion.12
  118.5 1.4 copy.89
  119.8 6.2 %all-to-all-start = ((bf16[16,128,1,256]{3,1,2,0:T(8,128)(2,1)}), bf16[16,128,1,256]{3,1,2,0:T(8,128)(2,1)S(1)}, u32[]{:S(2)}, u32[]{:S(2)}) async-start(bf16[16,128,1,256]{3,1,2,0:T(8,128)(2,1)} %copy.89), calls=%async_computation | async-start | bytes 2097152 | tf_op jit(solution)/shard_map/all_to_all | solution.py:124
  126.0 11.3 %collective-permute-done.10 = bf16[320,864]{1,0:T(8,128)(2,1)} collective-permute-done((bf16[320,864]{1,0:T(8,128)(2,1)}, bf16[320,864]{1,0:T(8,128)(2,1)}, u32[]{:S(2)}, u32[]{:S(2)}) %collective-permute-start.10) | collective-permute-done | bytes 552992 | tf_op jit(solution)/shard_map/ppermute | solution.py:59
  137.4 5.8 %collective-permute-start.11 = (bf16[320,864]{1,0:T(8,128)(2,1)}, bf16[320,864]{1,0:T(8,128)(2,1)}, u32[]{:S(2)}, u32[]{:S(2)}) collective-permute-start(bf16[320,864]{1,0:T(8,128)(2,1)} %collective-permute-done.10), channel_id=1, source_target_pairs={{0,120},{8,0},{16,8},{24,16},{32,24},{40,32},{48,40},{56,48},{64,5... | collective-permute-start | bytes 1658888 | tf_op jit(solution)/shard_map/ppermute | solution.py:59
  143.1 4.5 %collective-permute-done.4 = bf16[320,864]{1,0:T(8,128)(2,1)} collective-permute-done((bf16[320,864]{1,0:T(8,128)(2,1)}, bf16[320,864]{1,0:T(8,128)(2,1)}, u32[]{:S(2)}, u32[]{:S(2)}) %collective-permute-start.4) | collective-permute-done | bytes 552992 | tf_op jit(solution)/shard_map/ppermute | solution.py:57
  147.6 14.9 %collective-permute-done.11 = bf16[320,864]{1,0:T(8,128)(2,1)} collective-permute-done((bf16[320,864]{1,0:T(8,128)(2,1)}, bf16[320,864]{1,0:T(8,128)(2,1)}, u32[]{:S(2)}, u32[]{:S(2)}) %collective-permute-start.11) | collective-permute-done | bytes 552992 | tf_op jit(solution)/shard_map/ppermute | solution.py:59
  162.5 5.0 %collective-permute-start.12 = (bf16[320,864]{1,0:T(8,128)(2,1)}, bf16[320,864]{1,0:T(8,128)(2,1)}, u32[]{:S(2)}, u32[]{:S(2)}) collective-permute-start(bf16[320,864]{1,0:T(8,128)(2,1)} %collective-permute-done.11), channel_id=1, source_target_pairs={{0,120},{8,0},{16,8},{24,16},{32,24},{40,32},{48,40},{56,48},{64,5... | collective-permute-start | bytes 1658888 | tf_op jit(solution)/shard_map/ppermute | solution.py:59
  167.5 1.2 collective-permute-done.5
  170.2 8.5 %collective-permute-done.12 = bf16[320,864]{1,0:T(8,128)(2,1)} collective-permute-done((bf16[320,864]{1,0:T(8,128)(2,1)}, bf16[320,864]{1,0:T(8,128)(2,1)}, u32[]{:S(2)}, u32[]{:S(2)}) %collective-permute-start.12) | collective-permute-done | bytes 552992 | tf_op jit(solution)/shard_map/ppermute | solution.py:59
  178.7 5.5 %collective-permute-start.13 = (bf16[320,864]{1,0:T(8,128)(2,1)}, bf16[320,864]{1,0:T(8,128)(2,1)S(1)}, u32[]{:S(2)}, u32[]{:S(2)}) collective-permute-start(bf16[320,864]{1,0:T(8,128)(2,1)} %collective-permute-done.12), channel_id=1, source_target_pairs={{0,120},{8,0},{16,8},{24,16},{32,24},{40,32},{48,40},{56,48},{64,5... | collective-permute-start | bytes 1658888 | tf_op jit(solution)/shard_map/ppermute | solution.py:59
  184.2 5.8 %multiply_reduce_fusion = f32[512]{0:T(512)S(1)} fusion(bf16[512,5120]{1,0:T(8,128)(2,1)} %all-reduce.3.cloned.1.call-done, bf16[512,5120]{1,0:T(8,128)(2,1)} %param.24), kind=kLoop, calls=%fused_computation.1 | loop fusion | flops 13106688 | bytes 10487808 | tf_op jit(solution)/shard_map/reduce_sum | solution.py:30
  190.1 4.4 %collective-permute-done.13 = bf16[320,864]{1,0:T(8,128)(2,1)S(1)} collective-permute-done((bf16[320,864]{1,0:T(8,128)(2,1)}, bf16[320,864]{1,0:T(8,128)(2,1)S(1)}, u32[]{:S(2)}, u32[]{:S(2)}) %collective-permute-start.13) | collective-permute-done | bytes 552992 | tf_op jit(solution)/shard_map/ppermute | solution.py:59
  194.5 5.4 %collective-permute-start.14 = (bf16[320,864]{1,0:T(8,128)(2,1)S(1)}, bf16[320,864]{1,0:T(8,128)(2,1)S(1)}, u32[]{:S(2)}, u32[]{:S(2)}) collective-permute-start(bf16[320,864]{1,0:T(8,128)(2,1)S(1)} %collective-permute-done.13), channel_id=1, source_target_pairs={{0,120},{8,0},{16,8},{24,16},{32,24},{40,32},{48,40},{56,48},{64,5... | collective-permute-start | bytes 1658888 | tf_op jit(solution)/shard_map/ppermute | solution.py:59
  200.0 1.9 constant_dynamic-update-slice_fusion.31
  201.9 1.9 constant_dynamic-update-slice_fusion.30
  203.8 1.9 constant_dynamic-update-slice_fusion.29
  205.7 1.9 constant_dynamic-update-slice_fusion.28
  207.6 1.9 constant_dynamic-update-slice_fusion.27
  209.6 1.9 constant_dynamic-update-slice_fusion.26
  211.5 0.8 constant_dynamic-update-slice_fusion.25
  212.3 0.9 constant_dynamic-update-slice_fusion.24
  213.2 0.9 constant_dynamic-update-slice_fusion.23
  214.1 0.9 constant_dynamic-update-slice_fusion.22
  215.0 1.9 constant_dynamic-update-slice_fusion.21
  216.9 1.9 constant_dynamic-update-slice_fusion.20
  218.8 1.9 constant_dynamic-update-slice_fusion.19
  220.7 1.9 constant_dynamic-update-slice_fusion.18
  222.6 0.9 constant_dynamic-update-slice_fusion.17
  223.6 1.0 constant_dynamic-update-slice_fusion.16
  224.5 1.9 constant_dynamic-update-slice_fusion.15
  226.4 1.9 constant_dynamic-update-slice_fusion.14
  228.3 1.9 constant_dynamic-update-slice_fusion.13
  230.3 1.9 constant_dynamic-update-slice_fusion.12
  232.2 1.9 constant_dynamic-update-slice_fusion.11
  234.1 0.9 constant_dynamic-update-slice_fusion.10
  235.0 0.9 constant_dynamic-update-slice_fusion.9
  235.9 0.9 constant_dynamic-update-slice_fusion.8
  236.7 0.9 constant_dynamic-update-slice_fusion.7
  237.6 0.9 constant_dynamic-update-slice_fusion.6
  238.5 1.9 constant_dynamic-update-slice_fusion.5
  240.4 1.9 constant_dynamic-update-slice_fusion.4
  242.3 1.9 constant_dynamic-update-slice_fusion.3
  244.3 1.9 constant_dynamic-update-slice_fusion.2
  246.2 0.9 constant_dynamic-update-slice_fusion.1
  247.1 0.9 constant_dynamic-update-slice_fusion
  248.0 12.1 %fusion.63 = f32[512,864]{0,1:T(8,128)S(1)} fusion(bf16[5120,864]{1,0:T(8,128)(2,1)} %all-gather.2.cloned.1.call-done, bf16[512,5120]{1,0:T(8,128)(2,1)} %all-reduce.3.cloned.1.call-done, bf16[512,5120]{1,0:T(8,128)(2,1)} %param.24, f32[5120]{0:T(1024)S(1)} %copy-done.7, f32[512]{0:T(512)S(1)} %add_rsqrt_fusion), kind=kOutput, calls=%fused_computation.140 | convolution fusion | flops 4545576960 | bytes 21125120 | tf_op jit(solution)/shard_map/dot_general | solution.py:136
  260.0 13.4 %multiply_convert_fusion.1 = bf16[512,864]{0,1:T(8,128)(2,1)} fusion(f32[512,864]{0,1:T(8,128)S(1)} %fusion.63, bf16[10240,864]{1,0:T(8,128)(2,1)} %constant_dynamic-update-slice_fusion, s32[]{:T(128)S(6)} %select_n.108, bf16[512,5120]{1,0:T(8,128)(2,1)} %all-reduce.3.cloned.1.call-done, bf16[512,5120]{1,0:T(8,128)(2,1)} %param.24, f32[5120]{0:T(1024)S(1)} %copy-done.7, ...), kind=kOutput, calls=%fused_computation.13 | convolution fusion | flops 4548231168 | bytes 22337540 | tf_op jit(solution)/shard_map/dot_general | solution.py:137
  (68 shorter events, 11.7 us)
Async XLA Ops:
  8.0 176.2 %all-reduce.3.cloned.1.call-start = ((), (), s32[]{:S(2)}) async-start(), calls=%async_computation.1 | async-start | bytes 10485760 | tf_op jit(solution)/shard_map/psum | solution.py:132
  11.9 8.6 %copy-start = (bf16[384,5120]{1,0:T(8,128)(2,1)S(1)}, bf16[384,5120]{1,0:T(8,128)(2,1)}, u32[]{:S(2)}) copy-start(bf16[384,5120]{1,0:T(8,128)(2,1)} %param.23) | copy-start | bytes 11796484
  17.6 8.2 %copy-start.1 = (bf16[320,864]{1,0:T(8,128)(2,1)S(1)}, bf16[320,864]{1,0:T(8,128)(2,1)}, u32[]{:S(2)}) copy-start(bf16[320,864]{1,0:T(8,128)(2,1)} %param.27) | copy-start | bytes 1658884
  17.6 71.4 %copy-start.4 = (bf16[512,128]{1,0:T(8,128)(2,1)S(1)}, bf16[512,128]{1,0:T(8,128)(2,1)}, u32[]{:S(2)}) copy-start(bf16[512,128]{1,0:T(8,128)(2,1)} %param.16) | copy-start | bytes 393220
  17.6 71.4 %copy-start.6 = (f32[128]{0:T(128)S(1)}, f32[128]{0:T(128)}, u32[]{:S(2)}) copy-start(f32[128]{0:T(128)} %param.19) | copy-start | bytes 1540
  18.4 150.3 %copy-start.5 = (s32[16,4]{0,1:T(4,128)S(1)}, s32[16,4]{0,1:T(4,128)}, u32[]{:S(2)}) copy-start(s32[16,4]{0,1:T(4,128)} %param.22) | copy-start | bytes 772
  25.2 222.7 %all-gather.2.cloned.1.call-start = ((), (), s32[]{:S(2)}) async-start(), calls=%async_computation.2 | async-start | bytes 9748480 | tf_op jit(solution)/shard_map/all_gather | solution.py:72
  25.8 19.8 %collective-permute-start = (bf16[320,864]{1,0:T(8,128)(2,1)S(1)}, bf16[320,864]{1,0:T(8,128)(2,1)S(1)}, u32[]{:S(2)}, u32[]{:S(2)}) collective-permute-start(bf16[320,864]{1,0:T(8,128)(2,1)S(1)} %copy-done.1), channel_id=1, source_target_pairs={{0,8},{8,16},{16,24},{24,32},{32,40},{40,48},{48,56},{56,64},{64,7... | collective-permute-start | bytes 1658888 | tf_op jit(solution)/shard_map/ppermute | solution.py:57
  45.6 22.9 %collective-permute-start.1 = (bf16[320,864]{1,0:T(8,128)(2,1)S(1)}, bf16[320,864]{1,0:T(8,128)(2,1)S(1)}, u32[]{:S(2)}, u32[]{:S(2)}) collective-permute-start(bf16[320,864]{1,0:T(8,128)(2,1)S(1)} %collective-permute-done), channel_id=1, source_target_pairs={{0,8},{8,16},{16,24},{24,32},{32,40},{40,48},{48,56},{56,64},{64,7... | collective-permute-start | bytes 1658888 | tf_op jit(solution)/shard_map/ppermute | solution.py:57
  45.6 33.6 %collective-permute-start.8 = (bf16[320,864]{1,0:T(8,128)(2,1)S(1)}, bf16[320,864]{1,0:T(8,128)(2,1)S(1)}, u32[]{:S(2)}, u32[]{:S(2)}) collective-permute-start(bf16[320,864]{1,0:T(8,128)(2,1)S(1)} %copy-done.1), channel_id=1, source_target_pairs={{0,120},{8,0},{16,8},{24,16},{32,24},{40,32},{48,40},{56,48},{64,5... | collective-permute-start | bytes 1658888 | tf_op jit(solution)/shard_map/ppermute | solution.py:59
  68.5 19.7 %collective-permute-start.2 = (bf16[320,864]{1,0:T(8,128)(2,1)S(1)}, bf16[320,864]{1,0:T(8,128)(2,1)S(1)}, u32[]{:S(2)}, u32[]{:S(2)}) collective-permute-start(bf16[320,864]{1,0:T(8,128)(2,1)S(1)} %collective-permute-done.1), channel_id=1, source_target_pairs={{0,8},{8,16},{16,24},{24,32},{32,40},{40,48},{48,56},{56,64},{64,7... | collective-permute-start | bytes 1658888 | tf_op jit(solution)/shard_map/ppermute | solution.py:57
  79.3 29.3 %collective-permute-start.9 = (bf16[320,864]{1,0:T(8,128)(2,1)S(1)}, bf16[320,864]{1,0:T(8,128)(2,1)}, u32[]{:S(2)}, u32[]{:S(2)}) collective-permute-start(bf16[320,864]{1,0:T(8,128)(2,1)S(1)} %collective-permute-done.8), channel_id=1, source_target_pairs={{0,120},{8,0},{16,8},{24,16},{32,24},{40,32},{48,40},{56,48},{64,5... | collective-permute-start | bytes 1658888 | tf_op jit(solution)/shard_map/ppermute | solution.py:59
  88.2 31.7 %copy-start.2 = (bf16[320,864]{1,0:T(8,128)(2,1)}, bf16[320,864]{1,0:T(8,128)(2,1)S(1)}, u32[]{:S(2)}) copy-start(bf16[320,864]{1,0:T(8,128)(2,1)S(1)} %collective-permute-done.2) | copy-start | bytes 1658884
  88.2 28.7 %collective-permute-start.3 = (bf16[320,864]{1,0:T(8,128)(2,1)S(1)}, bf16[320,864]{1,0:T(8,128)(2,1)}, u32[]{:S(2)}, u32[]{:S(2)}) collective-permute-start(bf16[320,864]{1,0:T(8,128)(2,1)S(1)} %collective-permute-done.2), channel_id=1, source_target_pairs={{0,8},{8,16},{16,24},{24,32},{32,40},{40,48},{48,56},{56,64},{64,7... | collective-permute-start | bytes 1658888 | tf_op jit(solution)/shard_map/ppermute | solution.py:57
  108.6 28.8 %collective-permute-start.10 = (bf16[320,864]{1,0:T(8,128)(2,1)}, bf16[320,864]{1,0:T(8,128)(2,1)}, u32[]{:S(2)}, u32[]{:S(2)}) collective-permute-start(bf16[320,864]{1,0:T(8,128)(2,1)} %collective-permute-done.9), channel_id=1, source_target_pairs={{0,120},{8,0},{16,8},{24,16},{32,24},{40,32},{48,40},{56,48},{64,5... | collective-permute-start | bytes 1658888 | tf_op jit(solution)/shard_map/ppermute | solution.py:59
  116.9 30.7 %collective-permute-start.4 = (bf16[320,864]{1,0:T(8,128)(2,1)}, bf16[320,864]{1,0:T(8,128)(2,1)}, u32[]{:S(2)}, u32[]{:S(2)}) collective-permute-start(bf16[320,864]{1,0:T(8,128)(2,1)} %collective-permute-done.3), channel_id=1, source_target_pairs={{0,8},{8,16},{16,24},{24,32},{32,40},{40,48},{48,56},{56,64},{64,7... | collective-permute-start | bytes 1658888 | tf_op jit(solution)/shard_map/ppermute | solution.py:57
  119.8 48.9 %all-to-all-start = ((bf16[16,128,1,256]{3,1,2,0:T(8,128)(2,1)}), bf16[16,128,1,256]{3,1,2,0:T(8,128)(2,1)S(1)}, u32[]{:S(2)}, u32[]{:S(2)}) async-start(bf16[16,128,1,256]{3,1,2,0:T(8,128)(2,1)} %copy.89), calls=%async_computation | async-start | bytes 2097152 | tf_op jit(solution)/shard_map/all_to_all | solution.py:124
  137.4 25.2 %collective-permute-start.11 = (bf16[320,864]{1,0:T(8,128)(2,1)}, bf16[320,864]{1,0:T(8,128)(2,1)}, u32[]{:S(2)}, u32[]{:S(2)}) collective-permute-start(bf16[320,864]{1,0:T(8,128)(2,1)} %collective-permute-done.10), channel_id=1, source_target_pairs={{0,120},{8,0},{16,8},{24,16},{32,24},{40,32},{48,40},{56,48},{64,5... | collective-permute-start | bytes 1658888 | tf_op jit(solution)/shard_map/ppermute | solution.py:59
  147.6 21.1 %collective-permute-start.5 = (bf16[320,864]{1,0:T(8,128)(2,1)}, bf16[320,864]{1,0:T(8,128)(2,1)}, u32[]{:S(2)}, u32[]{:S(2)}) collective-permute-start(bf16[320,864]{1,0:T(8,128)(2,1)} %collective-permute-done.4), channel_id=1, source_target_pairs={{0,8},{8,16},{16,24},{24,32},{32,40},{40,48},{48,56},{56,64},{64,7... | collective-permute-start | bytes 1658888 | tf_op jit(solution)/shard_map/ppermute | solution.py:57
  162.5 16.2 %collective-permute-start.12 = (bf16[320,864]{1,0:T(8,128)(2,1)}, bf16[320,864]{1,0:T(8,128)(2,1)}, u32[]{:S(2)}, u32[]{:S(2)}) collective-permute-start(bf16[320,864]{1,0:T(8,128)(2,1)} %collective-permute-done.11), channel_id=1, source_target_pairs={{0,120},{8,0},{16,8},{24,16},{32,24},{40,32},{48,40},{56,48},{64,5... | collective-permute-start | bytes 1658888 | tf_op jit(solution)/shard_map/ppermute | solution.py:59
  168.7 15.6 %collective-permute-start.6 = (bf16[320,864]{1,0:T(8,128)(2,1)}, bf16[320,864]{1,0:T(8,128)(2,1)}, u32[]{:S(2)}, u32[]{:S(2)}) collective-permute-start(bf16[320,864]{1,0:T(8,128)(2,1)} %collective-permute-done.5), channel_id=1, source_target_pairs={{0,8},{8,16},{16,24},{24,32},{32,40},{40,48},{48,56},{56,64},{64,7... | collective-permute-start | bytes 1658888 | tf_op jit(solution)/shard_map/ppermute | solution.py:57
  169.5 64.6 %copy-start.3 = (bf16[320,864]{1,0:T(8,128)(2,1)S(1)}, bf16[320,864]{1,0:T(8,128)(2,1)}, u32[]{:S(2)}) copy-start(bf16[320,864]{1,0:T(8,128)(2,1)} %copy-done.2) | copy-start | bytes 1658884
  178.7 15.8 %collective-permute-start.13 = (bf16[320,864]{1,0:T(8,128)(2,1)}, bf16[320,864]{1,0:T(8,128)(2,1)S(1)}, u32[]{:S(2)}, u32[]{:S(2)}) collective-permute-start(bf16[320,864]{1,0:T(8,128)(2,1)} %collective-permute-done.12), channel_id=1, source_target_pairs={{0,120},{8,0},{16,8},{24,16},{32,24},{40,32},{48,40},{56,48},{64,5... | collective-permute-start | bytes 1658888 | tf_op jit(solution)/shard_map/ppermute | solution.py:59
  184.2 15.7 %collective-permute-start.7 = (bf16[320,864]{1,0:T(8,128)(2,1)}, bf16[320,864]{1,0:T(8,128)(2,1)}, u32[]{:S(2)}, u32[]{:S(2)}) collective-permute-start(bf16[320,864]{1,0:T(8,128)(2,1)} %collective-permute-done.6), channel_id=1, source_target_pairs={{0,8},{8,16},{16,24},{24,32},{32,40},{40,48},{48,56},{56,64},{64,7... | collective-permute-start | bytes 1658888 | tf_op jit(solution)/shard_map/ppermute | solution.py:57
  190.1 57.9 %copy-start.7 = (f32[5120]{0:T(1024)S(1)}, f32[5120]{0:T(1024)}, u32[]{:S(2)}) copy-start(f32[5120]{0:T(1024)} %param.25) | copy-start | bytes 61444
  194.5 29.0 %collective-permute-start.14 = (bf16[320,864]{1,0:T(8,128)(2,1)S(1)}, bf16[320,864]{1,0:T(8,128)(2,1)S(1)}, u32[]{:S(2)}, u32[]{:S(2)}) collective-permute-start(bf16[320,864]{1,0:T(8,128)(2,1)S(1)} %collective-permute-done.13), channel_id=1, source_target_pairs={{0,120},{8,0},{16,8},{24,16},{32,24},{40,32},{48,40},{56,48},{64,5... | collective-permute-start | bytes 1658888 | tf_op jit(solution)/shard_map/ppermute | solution.py:59
Sparse Core Ops, SparseCore 0:
  25.4 79.9 all-reduce.2
Sparse Core Ops, SparseCore 1:
  27.9 134.2 all-gather.1
